TPU v7x, 256 devices: a whole 4x4x8 slice. The times are simulated.
256 devices in a mesh: tok: 16 (over y, z_lo), wid: 16 (over z_hi, x, core).
Axes of the slice: x: 4, y: 4, z: 8 (z_hi: 2, z_lo: 4; z = z_hi * 4 + z_lo), core: 2. Of those that a mesh axis runs over, the one named last changes fastest.
Arguments:
- g_inverse: bfloat16 [16384, 16384], P('tok', 'wid'), may hold values from -1 to 18, as said below
- a_inverse: bfloat16 [16384, 16384], P('tok', 'wid'), may hold values from -1 to 18, as said below
- query_out: bfloat16 [16384, 128], P(('tok', 'wid')), may hold values from -0.046875 to 0.046875
- query_in: bfloat16 [16384, 128], P(('tok', 'wid')), may hold values from -0.01171875 to 0.01171875
- output_grads: bfloat16 [32768, 16384], P('tok', 'wid'), may hold values from -6 to 6
- activations: bfloat16 [32768, 16384], P('tok', 'wid'), may hold values from -6 to 6
Outputs:
- scores: float32 [8, 32768], P(None, ('tok', 'wid'))
Inputs may be any that keep to these rules, and one draw needn't show every extreme that they name: g_inverse is symmetric. a_inverse is symmetric.
All inputs are finite; a program needn't handle non-finite values.
Results may differ from a plain program's by a relative error of at most 0.0041.
Values may be sent and summed in bfloat16 or wider, within the bound.
A program may use at most 64 MiB of HBM per device.

v0:
```python
import jax
import jax.numpy as jnp
from jax import lax
from jax.sharding import PartitionSpec as P

QUERIES = 8
RANK = 16


def shards(g_inverse, a_inverse, query_out, query_in, output_grads, activations):
    width = g_inverse.shape[1]
    column = lax.axis_index("wid")
    full_out, full_in = (
        lax.all_gather(query_out, ("tok", "wid"), axis=0, tiled=True),
        lax.all_gather(query_in, ("tok", "wid"), axis=0, tiled=True),
    )
    slab_out = lax.dynamic_slice_in_dim(full_out, column * width, width, 0)
    slab_in = lax.dynamic_slice_in_dim(full_in, column * width, width, 0)
    part_out = jnp.dot(g_inverse, slab_out, preferred_element_type=jnp.float32)
    part_in = jnp.dot(a_inverse, slab_in, preferred_element_type=jnp.float32)
    sum_out, sum_in = lax.psum((part_out, part_in), "wid")
    whole_out, whole_in = (
        lax.all_gather(sum_out.astype(jnp.bfloat16), "tok", axis=0, tiled=True),
        lax.all_gather(sum_in.astype(jnp.bfloat16), "tok", axis=0, tiled=True),
    )
    g_pre = lax.dynamic_slice_in_dim(whole_out, column * width, width, 0)
    a_pre = lax.dynamic_slice_in_dim(whole_in, column * width, width, 0)
    out_part = jnp.dot(output_grads, g_pre, preferred_element_type=jnp.float32)
    in_part = jnp.dot(activations, a_pre, preferred_element_type=jnp.float32)
    share = output_grads.shape[0] // lax.axis_size("wid")
    total_out, total_in = lax.psum((out_part, in_part), "wid")
    out_proj = lax.dynamic_slice_in_dim(total_out, column * share, share, 0)
    in_proj = lax.dynamic_slice_in_dim(total_in, column * share, share, 0)
    product = out_proj * in_proj
    columns = product.shape[1]
    member = lax.broadcasted_iota(jnp.int32, (columns, QUERIES), 0) // RANK
    target = lax.broadcasted_iota(jnp.int32, (columns, QUERIES), 1)
    grouping = (member == target).astype(jnp.float32)
    return lax.dot_general(
        grouping,
        product,
        (((0,), (1,)), ((), ())),
        precision=lax.Precision.HIGHEST,
        preferred_element_type=jnp.float32,
    )


def solution(mesh):
    return jax.shard_map(
        shards,
        mesh=mesh,
        in_specs=(
            P("tok", "wid"),
            P("tok", "wid"),
            P(("tok", "wid"), None),
            P(("tok", "wid"), None),
            P("tok", "wid"),
            P("tok", "wid"),
        ),
        out_specs=P(None, ("tok", "wid")),
        check_vma=False,
    )
```

profile of v0, /device:TPU:2, one launch (start us, length us, event | category | flops | bytes accessed | tf_op | source)
XLA Modules:
  0.0 1332.6 jit_solution(992478465037619160)
XLA Ops:
  6.5 0.0 copy-start
  6.5 0.0 all-gather.5.cloned.1.call-start
  6.5 0.7 all-gather.5.cloned.1.call-update
  7.3 0.0 all-gather.9.cloned.1.call-start
  7.3 0.7 all-gather.9.cloned.1.call-update
  8.0 0.0 all-gather.11.cloned.1.call-start
  8.1 420.5 %all-gather.5.cloned.1.call-done = bf16[16384,128]{1,0:T(8,128)(2,1)} async-done(((bf16[64,128]{1,0:T(8,128)(2,1)}), bf16[16384,128]{1,0:T(8,128)(2,1)}) %all-gather.5.cloned.1.call-update) | async-done | bytes 4194320 | tf_op jit(solution)/shard_map/all_gather | solution.py:14
  428.5 0.0 copy-done
  428.5 1.8 convolution_bitcast_fusion.3
  430.3 414.6 %all-gather.9.cloned.1.call-done = bf16[16384,128]{1,0:T(8,128)(2,1)} async-done(((bf16[64,128]{1,0:T(8,128)(2,1)}), bf16[16384,128]{1,0:T(8,128)(2,1)}) %all-gather.9.cloned.1.call-update) | async-done | bytes 4194320 | tf_op jit(solution)/shard_map/all_gather | solution.py:15
  844.9 2.5 convolution_bitcast_fusion.2
  847.4 92.7 %all-reduce.6 = (bf16[1024,128]{0,1:T(8,128)(2,1)}, bf16[1024,128]{0,1:T(8,128)(2,1)}) all-reduce(f32[1024,128]{0,1:T(8,128)S(1)} %convolution_bitcast_fusion.2, f32[1024,128]{0,1:T(8,128)S(1)} %convolution_bitcast_fusion.3), channel_id=1, replica_groups=mesh['tok'=16,'wid'=16] {'wid'}, use_global_device_ids=true, to_apply=%region_2.0 | all-reduce | flops 262144 | bytes 1572864 | tf_op jit(solution)/shard_map/psum | solution.py:21
  940.1 0.0 all-gather.11.cloned.1.call-update
  940.1 0.0 all-gather.7.cloned.1.call-start
  940.2 0.5 all-gather.7.cloned.1.call-update
  940.7 0.0 all-reduce.5.cloned.1.call-start
  940.7 102.4 %all-gather.11.cloned.1.call-done = bf16[16384,128]{0,1:T(8,128)(2,1)} async-done(((bf16[1024,128]{0,1:T(8,128)(2,1)}), bf16[16384,128]{0,1:T(8,128)(2,1)}) %all-gather.11.cloned.1.call-update) | async-done | bytes 4194320 | tf_op jit(solution)/shard_map/all_gather | solution.py:24
  1043.1 4.9 convolution_bitcast_fusion
  1048.0 96.0 %all-gather.7.cloned.1.call-done = bf16[16384,128]{0,1:T(8,128)(2,1)} async-done(((bf16[1024,128]{0,1:T(8,128)(2,1)}), bf16[16384,128]{0,1:T(8,128)(2,1)}) %all-gather.7.cloned.1.call-update) | async-done | bytes 4194320 | tf_op jit(solution)/shard_map/all_gather | solution.py:23
  1144.0 4.8 convolution_bitcast_fusion.1
  1148.7 0.0 all-reduce.5.cloned.1.call-update
  1148.8 175.6 %all-reduce.5.cloned.1.call-done = (f32[2048,128]{0,1:T(8,128)}, f32[2048,128]{0,1:T(8,128)}) async-done(((f32[2048,128]{0,1:T(8,128)}, f32[2048,128]{0,1:T(8,128)}), (f32[2048,128]{0,1:T(8,128)}, f32[2048,128]{0,1:T(8,128)})) %all-reduce.5.cloned.1.call-update) | async-done | bytes 2097168 | tf_op jit(solution)/shard_map/psum | solution.py:31
  1324.3 1.8 fusion.4
  (2 shorter events, 0.0 us)
Async XLA Ops:
  6.5 422.0 %copy-start = (bf16[1024,1024]{1,0:T(8,128)(2,1)S(1)}, bf16[1024,1024]{1,0:T(8,128)(2,1)}, u32[]{:S(2)}) copy-start(bf16[1024,1024]{1,0:T(8,128)(2,1)} %param.6) | copy-start | bytes 6291460
  6.5 422.0 %all-gather.5.cloned.1.call-start = ((), (), s32[]{:S(2)}) async-start(), calls=%async_computation | async-start | bytes 4210688 | tf_op jit(solution)/shard_map/all_gather | solution.py:14
  7.3 837.6 %all-gather.9.cloned.1.call-start = ((), (), s32[]{:S(2)}) async-start(), calls=%async_computation.2 | async-start | bytes 4210688 | tf_op jit(solution)/shard_map/all_gather | solution.py:15
  8.0 1035.1 %all-gather.11.cloned.1.call-start = ((), (), s32[]{:S(2)}) async-start(), calls=%async_computation.3 | async-start | bytes 4456448 | tf_op jit(solution)/shard_map/all_gather | solution.py:24
  940.1 203.8 %all-gather.7.cloned.1.call-start = ((), (), s32[]{:S(2)}) async-start(), calls=%async_computation.1 | async-start | bytes 4456448 | tf_op jit(solution)/shard_map/all_gather | solution.py:23
  940.7 383.7 %all-reduce.5.cloned.1.call-start = ((), (), s32[]{:S(2)}) async-start(), calls=%async_computation.4 | async-start | bytes 4194304 | tf_op jit(solution)/shard_map/psum | solution.py:31
Sparse Core Ops, SparseCore 0:
  9.2 419.2 all-gather.4
  430.4 414.4 all-gather.8
  940.2 102.8 all-gather.10
  1044.8 99.1 all-gather.6
  1148.9 175.4 all-reduce.4
where the time goes:
time: 1340 us; the launch traced here: 1330 us
  waiting for transfers between devices  1210 us (90%)
  blocking collectives  92.7 us (7%)
  matrix products  15.7 us (1%)
    all_gather x1, waiting for transfers between devices, shards(): lax.all_gather(query_out, ('tok', 'wid'), axis=0, tiled=True)  420 us
    all_gather x1, waiting for transfers between devices, shards(): lax.all_gather(query_in, ('tok', 'wid'), axis=0, tiled=True)  415 us
    psum x1, waiting for transfers between devices, shards(): total_out, total_in = lax.psum((out_part, in_part), 'wid')  176 us
    all_gather x1, waiting for transfers between devices, shards(): lax.all_gather(sum_in.astype(jnp.bfloat16), 'tok', axis=0, tiled=True)  102 us
    all_gather x1, waiting for transfers between devices, shards(): lax.all_gather(sum_out.astype(jnp.bfloat16), 'tok', axis=0, tiled=True)  96 us
    psum x1, blocking collectives, shards(): sum_out, sum_in = lax.psum((part_out, part_in), 'wid')  92.7 us
  transfers between devices with their start and end apart: 5, of which 5 were waited for; matrix products, arithmetic and copies ran while one was open for 0% of the time, Pallas kernels for 0%

commit v1 on v0

v1 whole, which is shorter than its diff:
```python
import jax
import jax.numpy as jnp
from jax import lax
from jax.experimental import pallas as pl
from jax.experimental.pallas import tpu as pltpu
from jax.sharding import PartitionSpec as P

Y, Z, H, X, C = 4, 4, 2, 4, 2
QUERIES = 8
RANK = 16
COLS = QUERIES * RANK
BLOCK = 1024
TOKENS = 2048
PIECE = BLOCK // (H * X * C)
ROWS = COLS // Y
WIDE = BLOCK // Z
SHARE = TOKENS // (H * X * C)


def kernel(
    g_hbm, a_hbm, qo_hbm, qi_hbm, og_hbm, ac_hbm,
    out_ref,
    inv, tok, q, part, yin, zout, zin, pre, own, cout, cin, xout, xin, zhout, zhin,
    load_sem, a_send, a_recv, y_send, y_recv, z_send, z_recv, gz_send, gz_recv,
    gy_send, gy_recv, c_send, c_recv, x_send, x_recv, h_send, h_recv,
):
    my_tok, my_wid = lax.axis_index("tok"), lax.axis_index("wid")
    y, z = my_tok // Z, my_tok % Z
    h, x, c = my_wid // (X * C), (my_wid // C) % X, my_wid % C

    def at(dy=0, dz=0, dh=0, dx=0, dc=0):
        return (
            (y + dy) % Y * Z + (z + dz) % Z,
            (h + dh) % H * (X * C) + (x + dx) % X * C + (c + dc) % C,
        )

    sent = []

    def send(src, dst, send_sem, recv_sem, peer):
        copy = pltpu.make_async_remote_copy(
            src_ref=src, dst_ref=dst, send_sem=send_sem, recv_sem=recv_sem,
            device_id=peer, device_id_type=pl.DeviceIdType.MESH,
        )
        copy.start()
        sent.append(copy)
        return copy

    loads = [
        pltpu.make_async_copy(src, dst, load_sem.at[i])
        for i, (src, dst) in enumerate((
            (qo_hbm, q.at[my_wid, 0]),
            (qi_hbm, q.at[my_wid, 1]),
            (g_hbm, inv.at[0]),
            (a_hbm, inv.at[1]),
            (og_hbm, tok.at[0]),
            (ac_hbm, tok.at[1]),
        ))
    ]
    for load in loads:
        load.start()

    barrier = pltpu.get_barrier_semaphore()
    peers = (
        [at(dh=1), at(dc=1)]
        + [at(dx=d) for d in (1, 2, 3)]
        + [at(dy=d) for d in (1, 2, 3)]
        + [at(dz=d) for d in (1, 2, 3)]
    )
    for peer in peers:
        pl.semaphore_signal(barrier, inc=1, device_id=peer, device_id_type=pl.DeviceIdType.MESH)
    loads[0].wait()
    loads[1].wait()
    pl.semaphore_wait(barrier, len(peers))

    def spread(dh, dx, to_h, to_x, to_c):
        held = q.at[(h - dh) % H * (X * C) + (x - dx) % X * C + c]
        slot = (dh + to_h) * (X * C) + (dx + to_x) * C + to_c
        return send(held, held, a_send.at[slot], a_recv.at[slot], at(dh=to_h, dx=to_x, dc=to_c))

    arrive = {}
    arrive[1, 0, 0] = spread(0, 0, 1, 0, 0)
    for d in (2, 1, 3):
        arrive[0, d, 0] = spread(0, 0, 0, d, 0)
    arrive[0, 0, 1] = spread(0, 0, 0, 0, 1)
    for d in (1, 3, 2):
        arrive[0, d, 0].wait_recv()
        arrive[0, d, 1] = spread(0, d, 0, 0, 1)
    arrive[1, 0, 0].wait_recv()
    for d in (2, 1, 3):
        arrive[1, d, 0] = spread(1, 0, 0, d, 0)
    arrive[1, 0, 1] = spread(1, 0, 0, 0, 1)
    for d in (1, 3, 2):
        arrive[1, d, 0].wait_recv()
        arrive[1, d, 1] = spread(1, d, 0, 0, 1)
    for e in (0, 1):
        for d in range(X):
            arrive[e, d, 1].wait_recv()

    y_copy = {}
    for f in (0, 1):
        loads[2 + f].wait()
        query = q[:, f].reshape(BLOCK, COLS)
        for k in (1, 2, 3, 0):
            wide = pl.ds(pl.multiple_of((z + k) % Z * WIDE, WIDE), WIDE)
            term = lax.dot_general(
                query, inv[f, :, wide], (((0,), (0,)), ((), ())),
                preferred_element_type=jnp.float32,
            )
            part[f, k] = term.reshape(Y, ROWS, WIDE)
            for d in (2, 1, 3):
                y_copy[f, k, d] = send(
                    part.at[f, k, (y + d) % Y], yin.at[f, k, d - 1],
                    y_send.at[f, k, d - 1], y_recv.at[f, k, d - 1], at(dy=d),
                )

    z_copy = {}
    mine = {}
    for f in (0, 1):
        for k in (1, 2, 3, 0):
            for d in (1, 3, 2):
                y_copy[f, k, d].wait_recv()
            total = part[f, k, y] + ((yin[f, k, 0] + yin[f, k, 1]) + yin[f, k, 2])
            zout[f, k] = total
            if k:
                z_copy[f, k] = send(
                    zout.at[f, k], zin.at[f, k - 1],
                    z_send.at[f, k - 1], z_recv.at[f, k - 1], at(dz=k),
                )

    gz_copy, gy_copy = {}, {}

    def along_y(f, k):
        held = pre.at[f, (z - k) % Z, y]
        for d in (2, 1, 3):
            gy_copy[f, k, d] = send(
                held, held, gy_send.at[f, k, d - 1], gy_recv.at[f, k, d - 1], at(dy=d)
            )

    for f in (0, 1):
        for k in (1, 2, 3):
            z_copy[f, k].wait_recv()
        total = zout[f, 0] + ((zin[f, 0] + zin[f, 1]) + zin[f, 2])
        pre[f, z, y] = total.astype(jnp.bfloat16)
        held = pre.at[f, z, y]
        for k in (1, 2, 3):
            gz_copy[f, k] = send(
                held, held, gz_send.at[f, k - 1], gz_recv.at[f, k - 1], at(dz=k)
            )
        along_y(f, 0)
    for f in (0, 1):
        for k in (1, 2, 3):
            gz_copy[f, k].wait_recv()
            along_y(f, k)

    c_copy = {}
    for f in (0, 1):
        for k in range(Z):
            for d in (1, 3, 2):
                gy_copy[f, k, d].wait_recv()
        loads[4 + f].wait()
        for e in (1, 0):
            to = (h + e) % H
            for i in range(X):
                rows = pl.ds(pl.multiple_of((to * X + i) * (C * SHARE), C * SHARE), C * SHARE)
                proj = None
                for k in range(Z):
                    term = lax.dot_general(
                        pre[f, k].reshape(COLS, WIDE),
                        tok[f, rows, k * WIDE:(k + 1) * WIDE],
                        (((1,), (1,)), ((), ())),
                        preferred_element_type=jnp.float32,
                    )
                    proj = term if proj is None else proj + term
                low, high = proj[:, :SHARE], proj[:, SHARE:]
                first = c == 0
                own[f, e, i] = jnp.where(first, low, high)
                cout[f, e, i] = jnp.where(first, high, low).astype(jnp.bfloat16)
            c_copy[f, e] = send(
                cout.at[f, e], cin.at[f, e], c_send.at[f, e], c_recv.at[f, e], at(dc=1)
            )

    x_copy = {}
    for f in (0, 1):
        for e in (1, 0):
            c_copy[f, e].wait_recv()
            for d in (2, 1, 3):
                i = (x + d) % X
                xout[f, e, d - 1] = (own[f, e, i] + cin[f, e, i].astype(jnp.float32)).astype(jnp.bfloat16)
                x_copy[f, e, d] = send(
                    xout.at[f, e, d - 1], xin.at[f, e, d - 1],
                    x_send.at[f, e, d - 1], x_recv.at[f, e, d - 1], at(dx=d),
                )

    def over_x(f, e):
        for d in (1, 3, 2):
            x_copy[f, e, d].wait_recv()
        total = own[f, e, x] + cin[f, e, x].astype(jnp.float32)
        for d in (1, 2, 3):
            total = total + xin[f, e, d - 1].astype(jnp.float32)
        return total

    h_copy = {}
    for f in (0, 1):
        zhout[f] = over_x(f, 1).astype(jnp.bfloat16)
        h_copy[f] = send(zhout.at[f], zhin.at[f], h_send.at[f], h_recv.at[f], at(dh=1))
    proj = [over_x(f, 0) for f in (0, 1)]
    for f in (0, 1):
        h_copy[f].wait_recv()
        proj[f] = proj[f] + zhin[f].astype(jnp.float32)
    out_ref[...] = jnp.sum((proj[0] * proj[1]).reshape(QUERIES, RANK, SHARE), axis=1)
    for copy in sent:
        copy.wait_send()


def shards(*args):
    bf16, f32 = jnp.bfloat16, jnp.float32
    dma = pltpu.SemaphoreType.DMA
    pairs = lambda *shape: [dma(shape), dma(shape)]
    return pl.pallas_call(
        kernel,
        out_shape=jax.ShapeDtypeStruct((QUERIES, SHARE), f32),
        in_specs=[pl.BlockSpec(memory_space=pl.ANY)] * 6,
        out_specs=pl.BlockSpec(memory_space=pltpu.VMEM),
        scratch_shapes=[
            pltpu.VMEM((2, BLOCK, BLOCK), bf16),
            pltpu.VMEM((2, TOKENS, BLOCK), bf16),
            pltpu.VMEM((H * X * C, 2, PIECE, COLS), bf16),
            pltpu.VMEM((2, Z, Y, ROWS, WIDE), f32),
            pltpu.VMEM((2, Z, Y - 1, ROWS, WIDE), f32),
            pltpu.VMEM((2, Z, ROWS, WIDE), f32),
            pltpu.VMEM((2, Z - 1, ROWS, WIDE), f32),
            pltpu.VMEM((2, Z, Y, ROWS, WIDE), bf16),
            pltpu.VMEM((2, H, X, COLS, SHARE), f32),
            pltpu.VMEM((2, H, X, COLS, SHARE), bf16),
            pltpu.VMEM((2, H, X, COLS, SHARE), bf16),
            pltpu.VMEM((2, H, X - 1, COLS, SHARE), bf16),
            pltpu.VMEM((2, H, X - 1, COLS, SHARE), bf16),
            pltpu.VMEM((2, COLS, SHARE), bf16),
            pltpu.VMEM((2, COLS, SHARE), bf16),
            dma((6,)),
            *pairs(H * X * C),
            *pairs(2, Z, Y - 1),
            *pairs(2, Z - 1),
            *pairs(2, Z - 1),
            *pairs(2, Z, Y - 1),
            *pairs(2, H),
            *pairs(2, H, X - 1),
            *pairs(2),
        ],
        compiler_params=pltpu.CompilerParams(
            collective_id=0, has_side_effects=True, vmem_limit_bytes=60 << 20
        ),
    )(*args)


def solution(mesh):
    return jax.shard_map(
        shards,
        mesh=mesh,
        in_specs=(
            P("tok", "wid"),
            P("tok", "wid"),
            P(("tok", "wid"), None),
            P(("tok", "wid"), None),
            P("tok", "wid"),
            P("tok", "wid"),
        ),
        out_specs=P(None, ("tok", "wid")),
        check_vma=False,
    )
```

time: 1340 us -> 58.9 us (0.04)
  waiting for transfers between devices: 1210 us -> 0 us
  blocking collectives: 92.7 us -> 0 us
  Pallas kernels: 0 us -> 57.4 us
  matrix products: 15.7 us -> 0 us
    all_gather x4 -> x0, waiting for transfers between devices: 1030 us -> none  [the longest x1 420 us: shards(): lax.all_gather(query_out, ('tok', 'wid'), axis=0, tiled=True)]
    psum x1 -> x0, waiting for transfers between devices: 176 us -> none  [shards(): total_out, total_in = lax.psum((out_part, in_part), 'wid')]
    psum x1 -> x0, blocking collectives: 92.7 us -> none  [shards(): sum_out, sum_in = lax.psum((part_out, part_in), 'wid')]
    pallas_call x0 -> x1, Pallas kernels: none -> 57.4 us  [shards(): pl.pallas_call(kernel, out_shape=jax.ShapeDtypeStruct((QUERIES, SHARE), f...]
    dot_general x5 -> x0, matrix products: 15.7 us -> none  [the longest x1 4.85 us: shards(): in_part = jnp.dot(activations, a_pre, preferred_element_type=jnp.float32)]
  transfers between devices with their start and end apart: 5 -> 0, of which waited for: 5 -> 0; matrix products, arithmetic and copies ran while one was open for 0% -> 0% of each run, Pallas kernels for 0% -> 0%
where the time goes in v1:
time: 58.9 us; the launch traced here: 58.7 us
  Pallas kernels  57.4 us (97%)
  local copies, waits for them, and re-layouts  1.28 us (2%)
    pallas_call x1, Pallas kernels, shards(): pl.pallas_call(kernel, out_shape=jax.ShapeDtypeStruct((QUERIES, SHARE), f...  57.4 us
    unnamed x1, local copies, waits for them, and re-layouts  1.28 us

profile of v1, /device:TPU:2, one launch (start us, length us, event | category | flops | bytes accessed | tf_op | source)
XLA Modules:
  0.0 58.7 jit_solution(10546999957023354910)
XLA Ops:
  0.0 57.4 %shard_map.64 = f32[8,128]{1,0:T(8,128)} custom-call(bf16[1024,1024]{1,0:T(8,128)(2,1)} %g_hbm.1, bf16[1024,1024]{1,0:T(8,128)(2,1)} %a_hbm.1, bf16[64,128]{1,0:T(8,128)(2,1)} %qo_hbm.1, bf16[64,128]{1,0:T(8,128)(2,1)} %qi_hbm.1, bf16[2048,1024]{1,0:T(8,128)(2,1)} %og_hbm.1, bf16[2048,1024]{1,0:T(8,128)(2,1)} %ac_hbm.1), custom_call_target="tpu_custom_call" | custom-call | tf_op jit(solution)/shard_map/pallas_call | solution.py:219
  57.4 1.3 %copy.8 = f32[8,128]{1,0:T(8,128)} copy(f32[8,128]{1,0:T(8,128)} %shard_map.64) | data formatting | bytes 8192

commit v2 on v1

--- a/solution.py
+++ b/solution.py
@@ -12,7 +12,7 @@
 BLOCK = 1024
 TOKENS = 2048
 PIECE = BLOCK // (H * X * C)
-ROWS = COLS // Y
+ROWS = COLS // Y // 2
 WIDE = BLOCK // Z
 SHARE = TOKENS // (H * X * C)
 
@@ -20,7 +20,7 @@
 def kernel(
     g_hbm, a_hbm, qo_hbm, qi_hbm, og_hbm, ac_hbm,
     out_ref,
-    inv, tok, q, part, yin, zout, zin, pre, own, cout, cin, xout, xin, zhout, zhin,
+    inv, tok, q, part, yin, yout, zout, zin, pre, own, cout, cin, xout, xin, zhout, zhin,
     load_sem, a_send, a_recv, y_send, y_recv, z_send, z_recv, gz_send, gz_recv,
     gy_send, gy_recv, c_send, c_recv, x_send, x_recv, h_send, h_recv,
 ):
@@ -48,8 +48,8 @@
     loads = [
         pltpu.make_async_copy(src, dst, load_sem.at[i])
         for i, (src, dst) in enumerate((
-            (qo_hbm, q.at[my_wid, 0]),
-            (qi_hbm, q.at[my_wid, 1]),
+            (qo_hbm, q.at[0, my_wid]),
+            (qi_hbm, q.at[1, my_wid]),
             (g_hbm, inv.at[0]),
             (a_hbm, inv.at[1]),
             (og_hbm, tok.at[0]),
@@ -62,101 +62,140 @@
     barrier = pltpu.get_barrier_semaphore()
     peers = (
         [at(dh=1), at(dc=1)]
-        + [at(dx=d) for d in (1, 2, 3)]
-        + [at(dy=d) for d in (1, 2, 3)]
+        + [at(dx=d, dc=e) for d in (1, 2, 3) for e in (0, 1)]
+        + [at(dy=d) for d in (1, 3)]
+        + [at(dy=2)]
         + [at(dz=d) for d in (1, 2, 3)]
     )
     for peer in peers:
         pl.semaphore_signal(barrier, inc=1, device_id=peer, device_id_type=pl.DeviceIdType.MESH)
-    loads[0].wait()
-    loads[1].wait()
     pl.semaphore_wait(barrier, len(peers))
 
-    def spread(dh, dx, to_h, to_x, to_c):
-        held = q.at[(h - dh) % H * (X * C) + (x - dx) % X * C + c]
-        slot = (dh + to_h) * (X * C) + (dx + to_x) * C + to_c
-        return send(held, held, a_send.at[slot], a_recv.at[slot], at(dh=to_h, dx=to_x, dc=to_c))
-
-    arrive = {}
-    arrive[1, 0, 0] = spread(0, 0, 1, 0, 0)
-    for d in (2, 1, 3):
-        arrive[0, d, 0] = spread(0, 0, 0, d, 0)
-    arrive[0, 0, 1] = spread(0, 0, 0, 0, 1)
-    for d in (1, 3, 2):
-        arrive[0, d, 0].wait_recv()
-        arrive[0, d, 1] = spread(0, d, 0, 0, 1)
-    arrive[1, 0, 0].wait_recv()
-    for d in (2, 1, 3):
-        arrive[1, d, 0] = spread(1, 0, 0, d, 0)
-    arrive[1, 0, 1] = spread(1, 0, 0, 0, 1)
-    for d in (1, 3, 2):
-        arrive[1, d, 0].wait_recv()
-        arrive[1, d, 1] = spread(1, d, 0, 0, 1)
-    for e in (0, 1):
-        for d in range(X):
-            arrive[e, d, 1].wait_recv()
-
-    y_copy = {}
-    for f in (0, 1):
-        loads[2 + f].wait()
-        query = q[:, f].reshape(BLOCK, COLS)
-        for k in (1, 2, 3, 0):
-            wide = pl.ds(pl.multiple_of((z + k) % Z * WIDE, WIDE), WIDE)
-            term = lax.dot_general(
-                query, inv[f, :, wide], (((0,), (0,)), ((), ())),
-                preferred_element_type=jnp.float32,
-            )
-            part[f, k] = term.reshape(Y, ROWS, WIDE)
-            for d in (2, 1, 3):
-                y_copy[f, k, d] = send(
-                    part.at[f, k, (y + d) % Y], yin.at[f, k, d - 1],
-                    y_send.at[f, k, d - 1], y_recv.at[f, k, d - 1], at(dy=d),
+    a_copy = {}
+
+    def spread(f, src, dh, to_h, to_x, to_c):
+        slot = (dh + to_h) * (X * C) + to_x * C + to_c
+        a_copy[f, slot] = send(
+            src, q.at[f, (h - dh) % H * (X * C) + x * C + c],
+            a_send.at[f, slot], a_recv.at[f, slot], at(dh=to_h, dx=to_x, dc=to_c),
+        )
+
+    around = [(d, e) for d in (2, 1, 3) for e in (0, 1)] + [(0, 1)]
+    mine = (qo_hbm, qi_hbm)
+    for f in (0, 1):
+        spread(f, mine[f], 0, 1, 0, 0)
+    for f in (0, 1):
+        for d, e in around:
+            spread(f, mine[f], 0, 0, d, e)
+    for f in (0, 1):
+        a_copy[f, X * C].wait_recv()
+        for d, e in around:
+            spread(f, q.at[f, (h + 1) % H * (X * C) + x * C + c], 1, 0, d, e)
+
+    r_copy, d_copy, s_copy, z_copy, gz_copy, gy_copy = {}, {}, {}, {}, {}, {}
+    ORDER = (1, 2, 3, 0)
+
+    def way(s):
+        return 1 if s % 2 == 0 else -1
+
+    def factor_terms(s):
+        f, r = s // 2, s % 2
+        if r == 0:
+            loads[f].wait()
+            loads[2 + f].wait()
+            for slot in range(1, H * X * C):
+                if slot != X * C:
+                    a_copy[f, slot].wait_recv()
+            query = q[f].reshape(BLOCK, COLS)
+        for k in ORDER:
+            if r == 0:
+                wide = pl.ds(pl.multiple_of((z + k) % Z * WIDE, WIDE), WIDE)
+                term = lax.dot_general(
+                    query, inv[f, :, wide], (((0,), (0,)), ((), ())),
+                    preferred_element_type=jnp.float32,
+                ).reshape(Y, 2, ROWS, WIDE)
+                part[2 * f, k] = term[:, 0]
+                part[2 * f + 1, k] = term[:, 1]
+            r_copy[s, k] = send(
+                part.at[s, k, (y + 2) % Y], yin.at[s, k, 0],
+                y_send.at[s, k, 0], y_recv.at[s, k, 0], at(dy=way(s)),
+            )
+            d_copy[s, k] = send(
+                part.at[s, k, (y - way(s)) % Y], yin.at[s, k, 1],
+                y_send.at[s, k, 1], y_recv.at[s, k, 1], at(dy=-way(s)),
+            )
+
+    def relay(s):
+        for k in ORDER:
+            r_copy[s, k].wait_recv()
+            yout[s, k] = part[s, k, (y + way(s)) % Y] + yin[s, k, 0]
+            s_copy[s, k] = send(
+                yout.at[s, k], yin.at[s, k, 2],
+                y_send.at[s, k, 2], y_recv.at[s, k, 2], at(dy=way(s)),
+            )
+
+    def over_y(s):
+        for k in ORDER:
+            d_copy[s, k].wait_recv()
+            s_copy[s, k].wait_recv()
+            zout[s, k] = part[s, k, y] + (yin[s, k, 1] + yin[s, k, 2])
+            if k:
+                z_copy[s, k] = send(
+                    zout.at[s, k], zin.at[s, k - 1],
+                    z_send.at[s, k - 1], z_recv.at[s, k - 1], at(dz=k),
                 )
 
-    z_copy = {}
-    mine = {}
-    for f in (0, 1):
-        for k in (1, 2, 3, 0):
-            for d in (1, 3, 2):
-                y_copy[f, k, d].wait_recv()
-            total = part[f, k, y] + ((yin[f, k, 0] + yin[f, k, 1]) + yin[f, k, 2])
-            zout[f, k] = total
-            if k:
-                z_copy[f, k] = send(
-                    zout.at[f, k], zin.at[f, k - 1],
-                    z_send.at[f, k - 1], z_recv.at[f, k - 1], at(dz=k),
-                )
-
-    gz_copy, gy_copy = {}, {}
-
-    def along_y(f, k):
-        held = pre.at[f, (z - k) % Z, y]
+    def along_y(s, k):
+        held = pre.at[s // 2, (z - k) % Z, y, s % 2]
         for d in (2, 1, 3):
-            gy_copy[f, k, d] = send(
-                held, held, gy_send.at[f, k, d - 1], gy_recv.at[f, k, d - 1], at(dy=d)
-            )
-
-    for f in (0, 1):
+            gy_copy[s, k, d] = send(
+                held, held, gy_send.at[s, k, d - 1], gy_recv.at[s, k, d - 1], at(dy=d)
+            )
+
+    def over_z(s):
         for k in (1, 2, 3):
-            z_copy[f, k].wait_recv()
-        total = zout[f, 0] + ((zin[f, 0] + zin[f, 1]) + zin[f, 2])
-        pre[f, z, y] = total.astype(jnp.bfloat16)
-        held = pre.at[f, z, y]
+            z_copy[s, k].wait_recv()
+        total = zout[s, 0] + ((zin[s, 0] + zin[s, 1]) + zin[s, 2])
+        pre[s // 2, z, y, s % 2] = total.astype(jnp.bfloat16)
+        held = pre.at[s // 2, z, y, s % 2]
         for k in (1, 2, 3):
-            gz_copy[f, k] = send(
-                held, held, gz_send.at[f, k - 1], gz_recv.at[f, k - 1], at(dz=k)
-            )
-        along_y(f, 0)
-    for f in (0, 1):
+            gz_copy[s, k] = send(
+                held, held, gz_send.at[s, k - 1], gz_recv.at[s, k - 1], at(dz=k)
+            )
+        along_y(s, 0)
+
+    def onward(s):
         for k in (1, 2, 3):
-            gz_copy[f, k].wait_recv()
-            along_y(f, k)
+            gz_copy[s, k].wait_recv()
+            along_y(s, k)
+
+    factor_terms(0)
+    factor_terms(1)
+    factor_terms(2)
+    relay(0)
+    factor_terms(3)
+    relay(1)
+    over_y(0)
+    relay(2)
+    over_y(1)
+    over_z(0)
+    relay(3)
+    over_y(2)
+    over_z(1)
+    onward(0)
+    over_y(3)
+    over_z(2)
+    onward(1)
+    over_z(3)
+    onward(2)
+    onward(3)
 
     c_copy = {}
     for f in (0, 1):
-        for k in range(Z):
-            for d in (1, 3, 2):
-                gy_copy[f, k, d].wait_recv()
+        for s in (2 * f, 2 * f + 1):
+            for k in range(Z):
+                for d in (1, 3, 2):
+                    gy_copy[s, k, d].wait_recv()
         loads[4 + f].wait()
         for e in (1, 0):
             to = (h + e) % H
@@ -224,12 +263,13 @@
         scratch_shapes=[
             pltpu.VMEM((2, BLOCK, BLOCK), bf16),
             pltpu.VMEM((2, TOKENS, BLOCK), bf16),
-            pltpu.VMEM((H * X * C, 2, PIECE, COLS), bf16),
-            pltpu.VMEM((2, Z, Y, ROWS, WIDE), f32),
-            pltpu.VMEM((2, Z, Y - 1, ROWS, WIDE), f32),
-            pltpu.VMEM((2, Z, ROWS, WIDE), f32),
-            pltpu.VMEM((2, Z - 1, ROWS, WIDE), f32),
-            pltpu.VMEM((2, Z, Y, ROWS, WIDE), bf16),
+            pltpu.VMEM((2, H * X * C, PIECE, COLS), bf16),
+            pltpu.VMEM((4, Z, Y, ROWS, WIDE), f32),
+            pltpu.VMEM((4, Z, 3, ROWS, WIDE), f32),
+            pltpu.VMEM((4, Z, ROWS, WIDE), f32),
+            pltpu.VMEM((4, Z, ROWS, WIDE), f32),
+            pltpu.VMEM((4, Z - 1, ROWS, WIDE), f32),
+            pltpu.VMEM((2, Z, Y, 2, ROWS, WIDE), bf16),
             pltpu.VMEM((2, H, X, COLS, SHARE), f32),
             pltpu.VMEM((2, H, X, COLS, SHARE), bf16),
             pltpu.VMEM((2, H, X, COLS, SHARE), bf16),
@@ -238,11 +278,11 @@
             pltpu.VMEM((2, COLS, SHARE), bf16),
             pltpu.VMEM((2, COLS, SHARE), bf16),
             dma((6,)),
-            *pairs(H * X * C),
-            *pairs(2, Z, Y - 1),
-            *pairs(2, Z - 1),
-            *pairs(2, Z - 1),
-            *pairs(2, Z, Y - 1),
+            *pairs(2, H * X * C),
+            *pairs(4, Z, 3),
+            *pairs(4, Z - 1),
+            *pairs(4, Z - 1),
+            *pairs(4, Z, Y - 1),
             *pairs(2, H),
             *pairs(2, H, X - 1),
             *pairs(2),

time: 58.9 us -> 63 us (1.070)
  Pallas kernels: 57.4 us -> 61.6 us
    pallas_call x1, Pallas kernels: 57.4 us -> 61.6 us  [shards(): pl.pallas_call(kernel, out_shape=jax.ShapeDtypeStruct((QUERIES, SHARE), f...]
where the time goes in v2:
time: 63 us; the launch traced here: 62.8 us
  Pallas kernels  61.6 us (98%)
  local copies, waits for them, and re-layouts  1.28 us (2%)
    pallas_call x1, Pallas kernels, shards(): pl.pallas_call(kernel, out_shape=jax.ShapeDtypeStruct((QUERIES, SHARE), f...  61.6 us
    unnamed x1, local copies, waits for them, and re-layouts  1.28 us

profile of v2, /device:TPU:2, one launch (start us, length us, event | category | flops | bytes accessed | tf_op | source)
XLA Modules:
  0.0 62.8 jit_solution(5527251174367050424)
XLA Ops:
  0.0 61.6 %shard_map.64 = f32[8,128]{1,0:T(8,128)} custom-call(bf16[1024,1024]{1,0:T(8,128)(2,1)} %g_hbm.1, bf16[1024,1024]{1,0:T(8,128)(2,1)} %a_hbm.1, bf16[64,128]{1,0:T(8,128)(2,1)} %qo_hbm.1, bf16[64,128]{1,0:T(8,128)(2,1)} %qi_hbm.1, bf16[2048,1024]{1,0:T(8,128)(2,1)} %og_hbm.1, bf16[2048,1024]{1,0:T(8,128)(2,1)} %ac_hbm.1), custom_call_target="tpu_custom_call" | custom-call | tf_op jit(solution)/shard_map/pallas_call | solution.py:258
  61.6 1.3 %copy.8 = f32[8,128]{1,0:T(8,128)} copy(f32[8,128]{1,0:T(8,128)} %shard_map.64) | data formatting | bytes 8192

commit v3 on v1

v3 whole, which is shorter than its diff:
```python
import jax
import jax.numpy as jnp
from jax import lax
from jax.experimental import pallas as pl
from jax.experimental.pallas import tpu as pltpu
from jax.sharding import PartitionSpec as P

Y, Z, H, X, C = 4, 4, 2, 4, 2
QUERIES = 8
RANK = 16
COLS = QUERIES * RANK
BLOCK = 1024
TOKENS = 2048
PIECE = BLOCK // (H * X * C)
ROWS = COLS // Y
WIDE = BLOCK // Z
SHARE = TOKENS // (H * X * C)


def kernel(
    g_hbm, a_hbm, qo_hbm, qi_hbm, og_hbm, ac_hbm,
    out_ref,
    inv, tok, q, part, yin, zout, zin, pre, own, cout, cin, xout, xin, zhout, zhin,
    load_sem, a_send, a_recv, y_send, y_recv, z_send, z_recv, gz_send, gz_recv,
    gy_send, gy_recv, c_send, c_recv, x_send, x_recv, h_send, h_recv,
):
    f32, bf16 = jnp.float32, jnp.bfloat16
    my_tok, my_wid = lax.axis_index("tok"), lax.axis_index("wid")
    y, z = my_tok // Z, my_tok % Z
    h, x, c = my_wid // (X * C), (my_wid // C) % X, my_wid % C

    def at(dy=0, dz=0, dh=0, dx=0, dc=0):
        return (
            (y + dy) % Y * Z + (z + dz) % Z,
            (h + dh) % H * (X * C) + (x + dx) % X * C + (c + dc) % C,
        )

    def copy(src, dst, send_sem, recv_sem, peer):
        return pltpu.make_async_remote_copy(
            src_ref=src, dst_ref=dst, send_sem=send_sem, recv_sem=recv_sem,
            device_id=peer, device_id_type=pl.DeviceIdType.MESH,
        )

    def send(src, dst, send_sem, recv_sem, peer):
        copy(src, dst, send_sem, recv_sem, peer).start()

    def wait_recv(ref, sem):
        copy(ref, ref, load_sem.at[0], sem, at(dc=1)).wait_recv()

    def wait_send(ref, sem):
        copy(ref, ref, sem, load_sem.at[0], at(dc=1)).wait_send()

    loads = [
        pltpu.make_async_copy(src, dst, load_sem.at[i])
        for i, (src, dst) in enumerate((
            (qo_hbm, q.at[my_wid, 0]),
            (qi_hbm, q.at[my_wid, 1]),
            (g_hbm, inv.at[0]),
            (a_hbm, inv.at[1]),
            (og_hbm, tok.at[0]),
            (ac_hbm, tok.at[1]),
        ))
    ]
    for load in loads:
        load.start()

    around = [(d, e) for d in (2, 1, 3) for e in (0, 1)] + [(0, 1)]
    barrier = pltpu.get_barrier_semaphore()
    peers = (
        [at(dh=1)]
        + [at(dx=d, dc=e) for d, e in around]
        + [at(dy=d) for d in (2, 1, 3)]
        + [at(dz=d) for d in (1, 2, 3)]
    )
    for peer in peers:
        pl.semaphore_signal(barrier, inc=1, device_id=peer, device_id_type=pl.DeviceIdType.MESH)
    pl.semaphore_wait(barrier, len(peers))

    far = q.at[(my_wid + X * C) % (H * X * C)]
    mine = q.at[my_wid]
    for f, src in enumerate((qo_hbm, qi_hbm)):
        send(src, mine.at[f], a_send, a_recv.at[0], at(dh=1))
    loads[0].wait()
    loads[1].wait()
    for d, e in around:
        send(mine, mine, a_send, a_recv.at[1], at(dx=d, dc=e))
    wait_recv(far, a_recv.at[0])
    for d, e in around:
        send(far, far, a_send, a_recv.at[1], at(dx=d, dc=e))
    wait_recv(q.at[pl.ds(0, 2 * len(around))], a_recv.at[1])

    ORDER = (1, 2, 3, 0)
    for f in (0, 1):
        loads[2 + f].wait()
        query = q[:, f].reshape(BLOCK, COLS)
        for k in ORDER:
            wide = pl.ds(pl.multiple_of((z + k) % Z * WIDE, WIDE), WIDE)
            term = lax.dot_general(
                query, inv[f, :, wide], (((0,), (0,)), ((), ())), preferred_element_type=f32
            )
            part[f, k] = term.reshape(Y, ROWS, WIDE)
            for d in (2, 1, 3):
                send(
                    part.at[f, k, (y + d) % Y], yin.at[f, k, d - 1],
                    y_send, y_recv.at[f, k], at(dy=d),
                )

    def over_y(f, k):
        wait_recv(yin.at[f, k], y_recv.at[f, k])
        zout[f, k] = part[f, k, y] + ((yin[f, k, 0] + yin[f, k, 1]) + yin[f, k, 2])
        if k:
            send(zout.at[f, k], zin.at[f, k - 1], z_send, z_recv.at[f], at(dz=k))

    def along_y(f, k):
        held = pre.at[f, (z - k) % Z, y]
        for d in (2, 1, 3):
            send(held, held, gy_send.at[f], gy_recv.at[f], at(dy=d))

    def over_z(f):
        wait_recv(zin.at[f], z_recv.at[f])
        total = zout[f, 0] + ((zin[f, 0] + zin[f, 1]) + zin[f, 2])
        pre[f, z, y] = total.astype(bf16)
        held = pre.at[f, z, y]
        for k in (3, 2, 1):
            send(held, held, gz_send.at[f], gz_recv.at[f, k - 1], at(dz=k))
        along_y(f, 0)

    def onward(f):
        for k in (1, 2, 3):
            wait_recv(pre.at[f, 0, 0], gz_recv.at[f, k - 1])
            along_y(f, k)

    def project(f):
        wait_recv(pre.at[f, pl.ds(0, Y - 1)], gy_recv.at[f])
        loads[4 + f].wait()
        first = c == 0
        for e in (1, 0):
            to = (h + e) % H
            for i in range(X):
                rows = pl.ds(pl.multiple_of((to * X + i) * (C * SHARE), C * SHARE), C * SHARE)
                proj = None
                for k in range(Z):
                    term = lax.dot_general(
                        pre[f, k].reshape(COLS, WIDE),
                        tok[f, rows, k * WIDE:(k + 1) * WIDE],
                        (((1,), (1,)), ((), ())),
                        preferred_element_type=f32,
                    )
                    proj = term if proj is None else proj + term
                low, high = proj[:, :SHARE], proj[:, SHARE:]
                own[f, e, i] = jnp.where(first, low, high)
                cout[f, e, i] = jnp.where(first, high, low).astype(bf16)
            send(cout.at[f, e], cin.at[f, e], c_send, c_recv.at[f, e], at(dc=1))

    def along_x(f, e):
        wait_recv(cin.at[f, e], c_recv.at[f, e])
        for d in (2, 1, 3):
            i = (x + d) % X
            xout[f, e, d - 1] = (own[f, e, i] + cin[f, e, i].astype(f32)).astype(bf16)
            send(
                xout.at[f, e, d - 1], xin.at[f, e, d - 1],
                x_send, x_recv.at[f, e], at(dx=d),
            )

    def over_x(f, e):
        total = own[f, e, x] + cin[f, e, x].astype(f32)
        wait_recv(xin.at[f, e], x_recv.at[f, e])
        for d in (1, 2, 3):
            total = total + xin[f, e, d - 1].astype(f32)
        return total

    def along_h(f):
        zhout[f] = over_x(f, 1).astype(bf16)
        send(zhout.at[f], zhin.at[f], h_send, h_recv.at[f], at(dh=1))

    for k in ORDER:
        over_y(0, k)
    over_z(0)
    for k in ORDER[:3]:
        over_y(1, k)
    onward(0)
    over_y(1, 0)
    over_z(1)
    project(0)
    onward(1)
    along_x(0, 1)
    along_x(0, 0)
    wait_send(q.at[pl.ds(0, 2 * len(around) + 1)], a_send)
    wait_send(yin, y_send)
    wait_send(zin, z_send)
    project(1)
    along_h(0)
    along_x(1, 1)
    along_x(1, 0)
    wait_send(pre.at[0, pl.ds(0, Y - 1)], gy_send.at[0])
    wait_send(pre.at[1, pl.ds(0, Y - 1)], gy_send.at[1])
    for f in (0, 1):
        wait_send(pre.at[f, 0, pl.ds(0, Z - 1)], gz_send.at[f])
    along_h(1)
    wait_send(cout, c_send)
    proj = [over_x(f, 0) for f in (0, 1)]
    wait_send(xout, x_send)
    wait_send(zhout, h_send)
    for f in (0, 1):
        wait_recv(zhin.at[f], h_recv.at[f])
        proj[f] = proj[f] + zhin[f].astype(f32)
    out_ref[...] = jnp.sum((proj[0] * proj[1]).reshape(QUERIES, RANK, SHARE), axis=1)


def shards(*args):
    bf16, f32 = jnp.bfloat16, jnp.float32
    dma = pltpu.SemaphoreType.DMA
    return pl.pallas_call(
        kernel,
        out_shape=jax.ShapeDtypeStruct((QUERIES, SHARE), f32),
        in_specs=[pl.BlockSpec(memory_space=pl.ANY)] * 6,
        out_specs=pl.BlockSpec(memory_space=pltpu.VMEM),
        scratch_shapes=[
            pltpu.VMEM((2, BLOCK, BLOCK), bf16),
            pltpu.VMEM((2, TOKENS, BLOCK), bf16),
            pltpu.VMEM((H * X * C, 2, PIECE, COLS), bf16),
            pltpu.VMEM((2, Z, Y, ROWS, WIDE), f32),
            pltpu.VMEM((2, Z, Y - 1, ROWS, WIDE), f32),
            pltpu.VMEM((2, Z, ROWS, WIDE), f32),
            pltpu.VMEM((2, Z - 1, ROWS, WIDE), f32),
            pltpu.VMEM((2, Z, Y, ROWS, WIDE), bf16),
            pltpu.VMEM((2, H, X, COLS, SHARE), f32),
            pltpu.VMEM((2, H, X, COLS, SHARE), bf16),
            pltpu.VMEM((2, H, X, COLS, SHARE), bf16),
            pltpu.VMEM((2, H, X - 1, COLS, SHARE), bf16),
            pltpu.VMEM((2, H, X - 1, COLS, SHARE), bf16),
            pltpu.VMEM((2, COLS, SHARE), bf16),
            pltpu.VMEM((2, COLS, SHARE), bf16),
            dma((6,)),
            dma, dma((2,)),
            dma, dma((2, Z)),
            dma, dma((2,)),
            dma((2,)), dma((2, Z - 1)),
            dma((2,)), dma((2,)),
            dma, dma((2, H)),
            dma, dma((2, H)),
            dma, dma((2,)),
        ],
        compiler_params=pltpu.CompilerParams(
            collective_id=0, has_side_effects=True, vmem_limit_bytes=60 << 20
        ),
    )(*args)


def solution(mesh):
    return jax.shard_map(
        shards,
        mesh=mesh,
        in_specs=(
            P("tok", "wid"),
            P("tok", "wid"),
            P(("tok", "wid"), None),
            P(("tok", "wid"), None),
            P("tok", "wid"),
            P("tok", "wid"),
        ),
        out_specs=P(None, ("tok", "wid")),
        check_vma=False,
    )
```

time: 58.9 us -> 58 us (0.985)
  Pallas kernels: 57.4 us -> 56 us
    pallas_call x1, Pallas kernels: 57.4 us -> 56 us  [shards(): pl.pallas_call(kernel, out_shape=jax.ShapeDtypeStruct((QUERIES, SHARE), f...]
where the time goes in v3:
time: 58 us; the launch traced here: 57.3 us
  Pallas kernels  56 us (97%)
  local copies, waits for them, and re-layouts  1.28 us (2%)
    pallas_call x1, Pallas kernels, shards(): pl.pallas_call(kernel, out_shape=jax.ShapeDtypeStruct((QUERIES, SHARE), f...  56 us
    unnamed x1, local copies, waits for them, and re-layouts  1.28 us

profile of v3, /device:TPU:2, one launch (start us, length us, event | category | flops | bytes accessed | tf_op | source)
XLA Modules:
  0.0 57.3 jit_solution(14385684570198802074)
XLA Ops:
  0.0 56.0 %shard_map.64 = f32[8,128]{1,0:T(8,128)} custom-call(bf16[1024,1024]{1,0:T(8,128)(2,1)} %g_hbm.1, bf16[1024,1024]{1,0:T(8,128)(2,1)} %a_hbm.1, bf16[64,128]{1,0:T(8,128)(2,1)} %qo_hbm.1, bf16[64,128]{1,0:T(8,128)(2,1)} %qi_hbm.1, bf16[2048,1024]{1,0:T(8,128)(2,1)} %og_hbm.1, bf16[2048,1024]{1,0:T(8,128)(2,1)} %ac_hbm.1), custom_call_target="tpu_custom_call" | custom-call | tf_op jit(solution)/shard_map/pallas_call | solution.py:213
  56.0 1.3 %copy.8 = f32[8,128]{1,0:T(8,128)} copy(f32[8,128]{1,0:T(8,128)} %shard_map.64) | data formatting | bytes 8192

commit v4 on v3

v4 whole, which is shorter than its diff:
```python
import jax
import jax.numpy as jnp
from jax import lax
from jax.experimental import pallas as pl
from jax.experimental.pallas import tpu as pltpu
from jax.sharding import PartitionSpec as P

Y, Z, H, X, C = 4, 4, 2, 4, 2
QUERIES = 8
RANK = 16
COLS = QUERIES * RANK
BLOCK = 1024
TOKENS = 2048
PIECE = BLOCK // (H * X * C)
ROWS = COLS // Y // 2
WIDE = BLOCK // Z
SHARE = TOKENS // (H * X * C)


def kernel(
    g_hbm, a_hbm, qo_hbm, qi_hbm, og_hbm, ac_hbm,
    out_ref,
    inv, tok, q, part, yin, zout, zin, pre, own, cout, cin, xout, xin, zhout, zhin,
    load_sem, a_send, a_recv, y_send, y_recv, z_send, z_recv, gz_send, gz_recv,
    gy_send, gy_recv, c_send, c_recv, x_send, x_recv, h_send, h_recv,
):
    f32, bf16 = jnp.float32, jnp.bfloat16
    my_tok, my_wid = lax.axis_index("tok"), lax.axis_index("wid")
    y, z = my_tok // Z, my_tok % Z
    h, x, c = my_wid // (X * C), (my_wid // C) % X, my_wid % C

    other_z = (z, z + 1 - 2 * (z % 2), (z + 2) % Z, Z - 1 - z)

    def at(dy=0, dz=0, dh=0, dx=0, dc=0):
        return (
            (y + dy) % Y * Z + other_z[dz],
            (h + dh) % H * (X * C) + (x + dx) % X * C + (c + dc) % C,
        )

    def copy(src, dst, send_sem, recv_sem, peer):
        return pltpu.make_async_remote_copy(
            src_ref=src, dst_ref=dst, send_sem=send_sem, recv_sem=recv_sem,
            device_id=peer, device_id_type=pl.DeviceIdType.MESH,
        )

    def send(src, dst, send_sem, recv_sem, peer):
        copy(src, dst, send_sem, recv_sem, peer).start()

    def wait_recv(ref, sem):
        copy(ref, ref, load_sem.at[0], sem, at(dc=1)).wait_recv()

    def wait_send(ref, sem):
        copy(ref, ref, sem, load_sem.at[0], at(dc=1)).wait_send()

    loads = [
        pltpu.make_async_copy(src, dst, load_sem.at[i])
        for i, (src, dst) in enumerate((
            (qo_hbm, q.at[0, my_wid]),
            (qi_hbm, q.at[1, my_wid]),
            (g_hbm, inv.at[0]),
            (a_hbm, inv.at[1]),
            (og_hbm, tok.at[0]),
            (ac_hbm, tok.at[1]),
        ))
    ]
    for load in loads:
        load.start()

    around = [(d, e) for d in (2, 1, 3) for e in (0, 1)] + [(0, 1)]
    barrier = pltpu.get_barrier_semaphore()
    peers = (
        [at(dh=1)]
        + [at(dx=d, dc=e) for d, e in around]
        + [at(dy=d) for d in (2, 1, 3)]
        + [at(dz=d) for d in (1, 2, 3)]
    )
    for peer in peers:
        pl.semaphore_signal(barrier, inc=1, device_id=peer, device_id_type=pl.DeviceIdType.MESH)
    pl.semaphore_wait(barrier, len(peers))

    far = (my_wid + X * C) % (H * X * C)
    for f, src in enumerate((qo_hbm, qi_hbm)):
        send(src, q.at[f, my_wid], a_send, a_recv.at[f, 0], at(dh=1))
    for f, src in enumerate((qo_hbm, qi_hbm)):
        for d, e in around:
            send(src, q.at[f, my_wid], a_send, a_recv.at[f, 1], at(dx=d, dc=e))
    for f in (0, 1):
        wait_recv(q.at[f, far], a_recv.at[f, 0])
        for d, e in around:
            send(q.at[f, far], q.at[f, far], a_send, a_recv.at[f, 1], at(dx=d, dc=e))

    ORDER = (3, 2, 1, 0)

    def terms(f, first):
        loads[f].wait()
        loads[2 + f].wait()
        wait_recv(q.at[f, pl.ds(0, 2 * len(around))], a_recv.at[f, 1])
        query = q[f].reshape(BLOCK, COLS)
        for k in ORDER:
            wide = pl.ds(pl.multiple_of(other_z[k] * WIDE, WIDE), WIDE)
            term = lax.dot_general(
                query, inv[f, :, wide], (((0,), (0,)), ((), ())), preferred_element_type=f32
            ).reshape(Y, 2, ROWS, WIDE)
            part[2 * f, k] = term[:, 0]
            part[2 * f + 1, k] = term[:, 1]
            for s in first:
                share_out(s, k)

    def share_out(s, k):
        for d in (2, 1, 3):
            send(
                part.at[s, k, (y + d) % Y], yin.at[s, k, d - 1],
                y_send, y_recv.at[s, k], at(dy=d),
            )

    def share(s):
        for k in ORDER:
            share_out(s, k)

    def over_y(s):
        for k in ORDER:
            wait_recv(yin.at[s, k], y_recv.at[s, k])
            zout[s, k] = part[s, k, y] + ((yin[s, k, 0] + yin[s, k, 1]) + yin[s, k, 2])
            if k:
                send(zout.at[s, k], zin.at[s, k - 1], z_send, z_recv.at[s], at(dz=k))

    def along_y(s, k):
        held = pre.at[s // 2, other_z[k], y, s % 2]
        for d in (2, 1, 3):
            send(held, held, gy_send, gy_recv.at[s // 2], at(dy=d))

    def over_z(s):
        wait_recv(zin.at[s], z_recv.at[s])
        total = zout[s, 0] + ((zin[s, 0] + zin[s, 1]) + zin[s, 2])
        pre[s // 2, z, y, s % 2] = total.astype(bf16)
        held = pre.at[s // 2, z, y, s % 2]
        for k in (3, 2, 1):
            send(held, held, gz_send, gz_recv.at[s, k - 1], at(dz=k))
        along_y(s, 0)

    def onward(s):
        for k in (1, 2, 3):
            wait_recv(pre.at[0, 0, 0, 0], gz_recv.at[s, k - 1])
            along_y(s, k)

    def project(f, e):
        if e:
            wait_recv(pre.at[f, pl.ds(0, Y - 1)], gy_recv.at[f])
            loads[4 + f].wait()
        first = c == 0
        to = (h + e) % H
        for i in range(X):
            rows = pl.ds(pl.multiple_of((to * X + i) * (C * SHARE), C * SHARE), C * SHARE)
            proj = None
            for k in range(Z):
                term = lax.dot_general(
                    pre[f, k].reshape(COLS, WIDE),
                    tok[f, rows, k * WIDE:(k + 1) * WIDE],
                    (((1,), (1,)), ((), ())),
                    preferred_element_type=f32,
                )
                proj = term if proj is None else proj + term
            low, high = proj[:, :SHARE], proj[:, SHARE:]
            own[f, e, i] = jnp.where(first, low, high)
            cout[f, e, i] = jnp.where(first, high, low).astype(bf16)
        send(cout.at[f, e], cin.at[f, e], c_send, c_recv.at[f, e], at(dc=1))

    def along_x(f, e):
        wait_recv(cin.at[f, e], c_recv.at[f, e])
        for d in (2, 1, 3):
            i = (x + d) % X
            xout[f, e, d - 1] = (own[f, e, i] + cin[f, e, i].astype(f32)).astype(bf16)
            send(
                xout.at[f, e, d - 1], xin.at[f, e, d - 1],
                x_send, x_recv.at[f, e], at(dx=d),
            )

    def over_x(f, e):
        total = own[f, e, x] + cin[f, e, x].astype(f32)
        wait_recv(xin.at[f, e], x_recv.at[f, e])
        for d in (1, 2, 3):
            total = total + xin[f, e, d - 1].astype(f32)
        return total

    def along_h(f):
        zhout[f] = over_x(f, 1).astype(bf16)
        send(zhout.at[f], zhin.at[f], h_send, h_recv.at[f], at(dh=1))

    terms(0, (0,))
    share(1)
    terms(1, (2,))
    share(3)
    over_y(0)
    over_y(1)
    over_z(0)
    over_y(2)
    over_z(1)
    onward(0)
    over_y(3)
    over_z(2)
    onward(1)
    over_z(3)
    onward(2)
    onward(3)
    project(0, 1)
    project(0, 0)
    wait_send(q.at[:, pl.ds(0, 2 * len(around) + 1)], a_send)
    wait_send(yin, y_send)
    wait_send(zin, z_send)
    project(1, 1)
    along_x(0, 1)
    project(1, 0)
    along_x(1, 1)
    along_x(0, 0)
    along_x(1, 0)
    along_h(0)
    wait_send(pre.at[:, pl.ds(0, Y - 1)], gy_send)
    wait_send(pre.at[pl.ds(0, 1), pl.ds(0, 3)].at[:, :, pl.ds(0, 2)], gz_send)
    along_h(1)
    wait_send(cout, c_send)
    proj = [over_x(f, 0) for f in (0, 1)]
    wait_send(xout, x_send)
    wait_send(zhout, h_send)
    for f in (0, 1):
        wait_recv(zhin.at[f], h_recv.at[f])
        proj[f] = proj[f] + zhin[f].astype(f32)
    out_ref[...] = jnp.sum((proj[0] * proj[1]).reshape(QUERIES, RANK, SHARE), axis=1)


def shards(*args):
    bf16, f32 = jnp.bfloat16, jnp.float32
    dma = pltpu.SemaphoreType.DMA
    return pl.pallas_call(
        kernel,
        out_shape=pltpu.VMEM((QUERIES, SHARE), f32),
        in_specs=[pl.BlockSpec(memory_space=pl.ANY)] * 6,
        out_specs=pl.BlockSpec(memory_space=pltpu.VMEM),
        scratch_shapes=[
            pltpu.VMEM((2, BLOCK, BLOCK), bf16),
            pltpu.VMEM((2, TOKENS, BLOCK), bf16),
            pltpu.VMEM((2, H * X * C, PIECE, COLS), bf16),
            pltpu.VMEM((4, Z, Y, ROWS, WIDE), f32),
            pltpu.VMEM((4, Z, Y - 1, ROWS, WIDE), f32),
            pltpu.VMEM((4, Z, ROWS, WIDE), f32),
            pltpu.VMEM((4, Z - 1, ROWS, WIDE), f32),
            pltpu.VMEM((2, Z, Y, 2, ROWS, WIDE), bf16),
            pltpu.VMEM((2, H, X, COLS, SHARE), f32),
            pltpu.VMEM((2, H, X, COLS, SHARE), bf16),
            pltpu.VMEM((2, H, X, COLS, SHARE), bf16),
            pltpu.VMEM((2, H, X - 1, COLS, SHARE), bf16),
            pltpu.VMEM((2, H, X - 1, COLS, SHARE), bf16),
            pltpu.VMEM((2, COLS, SHARE), bf16),
            pltpu.VMEM((2, COLS, SHARE), bf16),
            dma((6,)),
            dma, dma((2, 2)),
            dma, dma((4, Z)),
            dma, dma((4,)),
            dma, dma((4, Z - 1)),
            dma, dma((2,)),
            dma, dma((2, H)),
            dma, dma((2, H)),
            dma, dma((2,)),
        ],
        compiler_params=pltpu.CompilerParams(
            collective_id=0, has_side_effects=True, vmem_limit_bytes=60 << 20
        ),
    )(*args)


def solution(mesh):
    return jax.shard_map(
        shards,
        mesh=mesh,
        in_specs=(
            P("tok", "wid"),
            P("tok", "wid"),
            P(("tok", "wid"), None),
            P(("tok", "wid"), None),
            P("tok", "wid"),
            P("tok", "wid"),
        ),
        out_specs=P(None, ("tok", "wid")),
        check_vma=False,
    )
```

time: 58 us -> 53.8 us (0.928)
  Pallas kernels: 56 us -> 52.5 us
  local copies, waits for them, and re-layouts: 1.28 us -> 0.6 us
    pallas_call x1, Pallas kernels: 56 us -> 52.5 us  [shards(): pl.pallas_call(kernel, out_shape=pltpu.VMEM((QUERIES, SHARE), f32), in_sp...]
    unnamed x1, local copies, waits for them, and re-layouts: 1.28 us -> 0.6 us
where the time goes in v4:
time: 53.8 us; the launch traced here: 53.1 us
  Pallas kernels  52.5 us (98%)
  local copies, waits for them, and re-layouts  0.6 us (1%)
    pallas_call x1, Pallas kernels, shards(): pl.pallas_call(kernel, out_shape=pltpu.VMEM((QUERIES, SHARE), f32), in_sp...  52.5 us

profile of v4, /device:TPU:2, one launch (start us, length us, event | category | flops | bytes accessed | tf_op | source)
XLA Modules:
  0.0 53.1 jit_solution(8941868451097640656)
XLA Ops:
  0.0 52.5 %shard_map.64 = f32[8,128]{1,0:T(8,128)S(1)} custom-call(bf16[1024,1024]{1,0:T(8,128)(2,1)} %g_hbm.1, bf16[1024,1024]{1,0:T(8,128)(2,1)} %a_hbm.1, bf16[64,128]{1,0:T(8,128)(2,1)} %qo_hbm.1, bf16[64,128]{1,0:T(8,128)(2,1)} %qi_hbm.1, bf16[2048,1024]{1,0:T(8,128)(2,1)} %og_hbm.1, bf16[2048,1024]{1,0:T(8,128)(2,1)} %ac_hbm.1), custom_call_target="tpu_custom_call" | custom-call | tf_op jit(solution)/shard_map/pallas_call | solution.py:233
  52.5 0.6 %copy.8 = f32[8,128]{1,0:T(8,128)} copy(f32[8,128]{1,0:T(8,128)S(1)} %shard_map.64) | data formatting | bytes 8192

commit v5 on v4

--- a/solution.py
+++ b/solution.py
@@ -20,8 +20,8 @@
 def kernel(
     g_hbm, a_hbm, qo_hbm, qi_hbm, og_hbm, ac_hbm,
     out_ref,
-    inv, tok, q, part, yin, zout, zin, pre, own, cout, cin, xout, xin, zhout, zhin,
-    load_sem, a_send, a_recv, y_send, y_recv, z_send, z_recv, gz_send, gz_recv,
+    inv, tok, q, part, yin, pin, two, zout, zin, pre, own, cout, cin, xout, xin, zhout, zhin,
+    load_sem, a_send, a_recv, y_send, y_recv, p_send, p_recv, z_send, z_recv, gz_send, gz_recv,
     gy_send, gy_recv, c_send, c_recv, x_send, x_recv, h_send, h_recv,
 ):
     f32, bf16 = jnp.float32, jnp.bfloat16
@@ -90,13 +90,14 @@
             send(q.at[f, far], q.at[f, far], a_send, a_recv.at[f, 1], at(dx=d, dc=e))
 
     ORDER = (3, 2, 1, 0)
+    PAIRED = (3,)
 
     def terms(f, first):
         loads[f].wait()
         loads[2 + f].wait()
         wait_recv(q.at[f, pl.ds(0, 2 * len(around))], a_recv.at[f, 1])
         query = q[f].reshape(BLOCK, COLS)
-        for k in ORDER:
+        for k in (ORDER if f == 0 else (3, 1, 2, 0)):
             wide = pl.ds(pl.multiple_of(other_z[k] * WIDE, WIDE), WIDE)
             term = lax.dot_general(
                 query, inv[f, :, wide], (((0,), (0,)), ((), ())), preferred_element_type=f32
@@ -105,24 +106,46 @@
             part[2 * f + 1, k] = term[:, 1]
             for s in first:
                 share_out(s, k)
+            if f == 1 and k == 1:
+                for s in PAIRED:
+                    for j in (1, 0):
+                        send(
+                            part.at[s, 2 * j + 1], pin.at[s - 2, j],
+                            p_send.at[s - 2], p_recv.at[s - 2, j], at(dz=1),
+                        )
 
     def share_out(s, k):
         for d in (2, 1, 3):
             send(
                 part.at[s, k, (y + d) % Y], yin.at[s, k, d - 1],
-                y_send, y_recv.at[s, k], at(dy=d),
+                y_send.at[s], y_recv.at[s, k], at(dy=d),
             )
 
     def share(s):
         for k in ORDER:
             share_out(s, k)
 
+    def pair(s):
+        for k in (2, 0):
+            j = k // 2
+            wait_recv(pin.at[s - 2, j], p_recv.at[s - 2, j])
+            two[s - 2, j] = part[s, k] + pin[s - 2, j]
+            for d in (2, 1, 3):
+                send(
+                    two.at[s - 2, j, (y + d) % Y], yin.at[s, k, d - 1],
+                    y_send.at[s], y_recv.at[s, k], at(dy=d),
+                )
+
     def over_y(s):
-        for k in ORDER:
+        for k in ((2, 0) if s in PAIRED else ORDER):
             wait_recv(yin.at[s, k], y_recv.at[s, k])
-            zout[s, k] = part[s, k, y] + ((yin[s, k, 0] + yin[s, k, 1]) + yin[s, k, 2])
+            mine = two[s - 2, k // 2, y] if s in PAIRED else part[s, k, y]
+            zout[s, k] = mine + ((yin[s, k, 0] + yin[s, k, 1]) + yin[s, k, 2])
             if k:
-                send(zout.at[s, k], zin.at[s, k - 1], z_send, z_recv.at[s], at(dz=k))
+                send(
+                    zout.at[s, k], zin.at[s, k - 1],
+                    z_send.at[s], z_recv.at[s], at(dz=k),
+                )
 
     def along_y(s, k):
         held = pre.at[s // 2, other_z[k], y, s % 2]
@@ -130,8 +153,12 @@
             send(held, held, gy_send, gy_recv.at[s // 2], at(dy=d))
 
     def over_z(s):
-        wait_recv(zin.at[s], z_recv.at[s])
-        total = zout[s, 0] + ((zin[s, 0] + zin[s, 1]) + zin[s, 2])
+        if s not in PAIRED:
+            wait_recv(zin.at[s], z_recv.at[s])
+            total = zout[s, 0] + ((zin[s, 0] + zin[s, 1]) + zin[s, 2])
+        else:
+            wait_recv(zin.at[s, 1], z_recv.at[s])
+            total = zout[s, 0] + zin[s, 1]
         pre[s // 2, z, y, s % 2] = total.astype(bf16)
         held = pre.at[s // 2, z, y, s % 2]
         for k in (3, 2, 1):
@@ -189,8 +216,8 @@
     terms(0, (0,))
     share(1)
     terms(1, (2,))
-    share(3)
     over_y(0)
+    pair(3)
     over_y(1)
     over_z(0)
     over_y(2)
@@ -205,15 +232,21 @@
     project(0, 1)
     project(0, 0)
     wait_send(q.at[:, pl.ds(0, 2 * len(around) + 1)], a_send)
-    wait_send(yin, y_send)
-    wait_send(zin, z_send)
+    for s in range(4):
+        if s in PAIRED:
+            wait_send(pin.at[s - 2], p_send.at[s - 2])
+            wait_send(yin.at[s, pl.ds(0, 2)], y_send.at[s])
+            wait_send(zin.at[s, 1], z_send.at[s])
+        else:
+            wait_send(yin.at[s], y_send.at[s])
+            wait_send(zin.at[s], z_send.at[s])
+    along_x(0, 1)
+    along_x(0, 0)
     project(1, 1)
-    along_x(0, 1)
     project(1, 0)
     along_x(1, 1)
-    along_x(0, 0)
+    along_h(0)
     along_x(1, 0)
-    along_h(0)
     wait_send(pre.at[:, pl.ds(0, Y - 1)], gy_send)
     wait_send(pre.at[pl.ds(0, 1), pl.ds(0, 3)].at[:, :, pl.ds(0, 2)], gz_send)
     along_h(1)
@@ -241,6 +274,8 @@
             pltpu.VMEM((2, H * X * C, PIECE, COLS), bf16),
             pltpu.VMEM((4, Z, Y, ROWS, WIDE), f32),
             pltpu.VMEM((4, Z, Y - 1, ROWS, WIDE), f32),
+            pltpu.VMEM((2, 2, Y, ROWS, WIDE), f32),
+            pltpu.VMEM((2, 2, Y, ROWS, WIDE), f32),
             pltpu.VMEM((4, Z, ROWS, WIDE), f32),
             pltpu.VMEM((4, Z - 1, ROWS, WIDE), f32),
             pltpu.VMEM((2, Z, Y, 2, ROWS, WIDE), bf16),
@@ -253,8 +288,9 @@
             pltpu.VMEM((2, COLS, SHARE), bf16),
             dma((6,)),
             dma, dma((2, 2)),
-            dma, dma((4, Z)),
-            dma, dma((4,)),
+            dma((4,)), dma((4, Z)),
+            dma((2,)), dma((2, 2)),
+            dma((4,)), dma((4,)),
             dma, dma((4, Z - 1)),
             dma, dma((2,)),
             dma, dma((2, H)),

time: 53.8 us -> 52.5 us (0.976)
  Pallas kernels: 52.5 us -> 51.6 us
    pallas_call x1, Pallas kernels: 52.5 us -> 51.6 us  [shards(): pl.pallas_call(kernel, out_shape=pltpu.VMEM((QUERIES, SHARE), f32), in_sp...]
where the time goes in v5:
time: 52.5 us; the launch traced here: 52.2 us
  Pallas kernels  51.6 us (98%)
  local copies, waits for them, and re-layouts  0.6 us (1%)
    pallas_call x1, Pallas kernels, shards(): pl.pallas_call(kernel, out_shape=pltpu.VMEM((QUERIES, SHARE), f32), in_sp...  51.6 us

profile of v5, /device:TPU:2, one launch (start us, length us, event | category | flops | bytes accessed | tf_op | source)
XLA Modules:
  0.0 52.2 jit_solution(272655859044208855)
XLA Ops:
  0.0 51.6 %shard_map.64 = f32[8,128]{1,0:T(8,128)S(1)} custom-call(bf16[1024,1024]{1,0:T(8,128)(2,1)} %g_hbm.1, bf16[1024,1024]{1,0:T(8,128)(2,1)} %a_hbm.1, bf16[64,128]{1,0:T(8,128)(2,1)} %qo_hbm.1, bf16[64,128]{1,0:T(8,128)(2,1)} %qi_hbm.1, bf16[2048,1024]{1,0:T(8,128)(2,1)} %og_hbm.1, bf16[2048,1024]{1,0:T(8,128)(2,1)} %ac_hbm.1), custom_call_target="tpu_custom_call" | custom-call | tf_op jit(solution)/shard_map/pallas_call | solution.py:266
  51.6 0.6 %copy.8 = f32[8,128]{1,0:T(8,128)} copy(f32[8,128]{1,0:T(8,128)S(1)} %shard_map.64) | data formatting | bytes 8192

commit v6 on v5

--- a/solution.py
+++ b/solution.py
@@ -63,9 +63,6 @@
             (ac_hbm, tok.at[1]),
         ))
     ]
-    for load in loads:
-        load.start()
-
     around = [(d, e) for d in (2, 1, 3) for e in (0, 1)] + [(0, 1)]
     barrier = pltpu.get_barrier_semaphore()
     peers = (
@@ -76,6 +73,8 @@
     )
     for peer in peers:
         pl.semaphore_signal(barrier, inc=1, device_id=peer, device_id_type=pl.DeviceIdType.MESH)
+    for load in loads:
+        load.start()
     pl.semaphore_wait(barrier, len(peers))
 
     far = (my_wid + X * C) % (H * X * C)

time: 52.5 us -> 52.9 us (level)
  Pallas kernels: 51.6 us -> 52.3 us
    pallas_call x1, Pallas kernels: 51.6 us -> 52.3 us  [shards(): pl.pallas_call(kernel, out_shape=pltpu.VMEM((QUERIES, SHARE), f32), in_sp...]
where the time goes in v6:
time: 52.9 us
  Pallas kernels  52.3 us (99%)
  local copies, waits for them, and re-layouts  0.6 us (1%)
    pallas_call x1, Pallas kernels, shards(): pl.pallas_call(kernel, out_shape=pltpu.VMEM((QUERIES, SHARE), f32), in_sp...  52.3 us

profile of v6, /device:TPU:2, one launch (start us, length us, event | category | flops | bytes accessed | tf_op | source)
XLA Modules:
  0.0 52.9 jit_solution(7364299499874888570)
XLA Ops:
  0.0 52.3 %shard_map.64 = f32[8,128]{1,0:T(8,128)S(1)} custom-call(bf16[1024,1024]{1,0:T(8,128)(2,1)} %g_hbm.1, bf16[1024,1024]{1,0:T(8,128)(2,1)} %a_hbm.1, bf16[64,128]{1,0:T(8,128)(2,1)} %qo_hbm.1, bf16[64,128]{1,0:T(8,128)(2,1)} %qi_hbm.1, bf16[2048,1024]{1,0:T(8,128)(2,1)} %og_hbm.1, bf16[2048,1024]{1,0:T(8,128)(2,1)} %ac_hbm.1), custom_call_target="tpu_custom_call" | custom-call | tf_op jit(solution)/shard_map/pallas_call | solution.py:265
  52.3 0.6 %copy.8 = f32[8,128]{1,0:T(8,128)} copy(f32[8,128]{1,0:T(8,128)S(1)} %shard_map.64) | data formatting | bytes 8192
